TPU v7x, 32 devices: a whole 2x2x4 slice. The times are simulated.
32 devices in a mesh: space: 4 (over y, core), shard: 8 (over z, x).
Axes of the slice: x: 2, y: 2, z: 4, core: 2. Of those that a mesh axis runs over, the one named last changes fastest.
Arguments:
- volume_field: float32 [2, 16, 16, 128, 128], P(None, None, 'space', 'shard'), may hold values from -6 to 6
- source: float32 [2, 16, 16, 128, 128], P(None, None, 'space', 'shard'), may hold values from -6 to 6
- material: int32 [16, 128, 128], P('space', 'shard'), may hold values from 0 to 7
- mat_real: float32 [8], replicated, may hold values from 0.5 to 4
- mat_loss: float32 [8], replicated, may hold values from 0.1 to 1.5
- surface_map: int32 [512, 128], P(('space', 'shard')), may hold values from 0 to 8191
- near_boxes: int32 [512, 4], P(('space', 'shard')), may hold values from 0 to 511, as said below
- near_blocks: bfloat16 [4, 256, 256], replicated, may hold values from -0.1875 to 0.1875
- radiate: bfloat16 [2, 128, 512], replicated, may hold values from -0.375 to 0.375
- interp: bfloat16 [512, 2048], replicated, may hold values from -0.25 to 0.25
- phase_angle: float32 [8, 2048], replicated, may hold values from -3.140625 to 3.140625
- far_parents: int32 [64, 8], replicated, may hold values from 0 to 63
- far_kind: int32 [64, 8], replicated, may hold values from 0 to 315
- translate: float32 [316, 2, 2048], P(None, None, 'shard'), may hold values from -0.18 to 0.18
Outputs:
- volume_out: float32 [2, 16, 16, 128, 128], P(None, None, 'space', 'shard')
- forcing: float32 [512, 16, 256], P(('space', 'shard'))
Inputs may be any that keep to these rules, and one draw needn't show every extreme that they name: near_boxes[b, 0] = b; every other entry is a box of the same group of 128 boxes (boxes g * 128 to (g + 1) * 128 - 1) whose index lies from 16 below to 31 above the first box of b's run of 16 boxes.
All inputs are finite; a program needn't handle non-finite values.
Results may differ from a plain program's by a relative error of at most 0.015.
Values may be sent and summed in bfloat16 or wider, within the bound.
No kernel may reach another device: no remote copies, remote signals or barrier semaphores. Data moves between devices by JAX's collectives and lax.ppermute only.
A program may use at most 128 MiB of HBM per device.

v0:
```python
import math
import jax
import jax.numpy as jnp
from jax import lax
from jax.sharding import PartitionSpec as P

relaxation = 0.8


def padded_2(array, sides, width):
    for axis, dim in sides:
        peers, length = (lax.axis_size(axis), array.shape[dim])
        up = [(i, (i + 1) % peers) for i in range(peers - 1)]
        down = [(j, i) for i, j in up]
        last = lax.slice_in_dim(array, length - width, length, axis=dim)
        leading = lax.slice_in_dim(array, 0, width, axis=dim)
        before = lax.ppermute(last, axis, up)
        after = lax.ppermute(leading, axis, down)
        array = jnp.concatenate([before, array, after], axis=dim)
    return array


def neighbour_sum(padded):
    core = padded[:, :, 1:-1, 1:-1]
    result = padded[:, :, 2:, 1:-1] + padded[:, :, :-2, 1:-1]
    result = result + padded[:, :, 1:-1, 2:] + padded[:, :, 1:-1, :-2]
    zero_layer = jnp.zeros(core.shape[:-1] + (1,), core.dtype)
    upper = jnp.concatenate([core[..., 1:], zero_layer], axis=-1)
    lower = jnp.concatenate([zero_layer, core[..., :-1]], axis=-1)
    return result + upper + lower


def relax_sweep(current, neighbours, source, diagonal_coef, loss_coef):
    real_part = diagonal_coef * current[0] - neighbours[0] - loss_coef * current[1]
    imag_part = diagonal_coef * current[1] - neighbours[1] + loss_coef * current[0]
    applied = jnp.stack([real_part, imag_part])
    return current + relaxation * (source - applied) / diagonal_coef


def block_matrix(radiate):
    upper = jnp.concatenate([radiate[0], radiate[1]], axis=1)
    lower = jnp.concatenate([-radiate[1], radiate[0]], axis=1)
    return jnp.concatenate([upper, lower], axis=0)


def aggregate(leaf_rows, interp, cosine, sine_part):
    parent_count = leaf_rows.shape[0] // 8
    excite = leaf_rows.shape[1]
    spread = jnp.dot(
        leaf_rows.reshape(-1, interp.shape[0]), interp, preferred_element_type=jnp.float32
    )
    spread = spread.reshape(parent_count, 8, excite, 2, interp.shape[1])
    cosine_wide = cosine[None, :, None, :]
    sine_wide = sine_part[None, :, None, :]
    real_part = jnp.sum(cosine_wide * spread[:, :, :, 0] - sine_wide * spread[:, :, :, 1], axis=1)
    imag_part = jnp.sum(sine_wide * spread[:, :, :, 0] + cosine_wide * spread[:, :, :, 1], axis=1)
    return jnp.stack([real_part, imag_part], axis=2).astype(jnp.bfloat16)


def combine_far(sources, table):
    real_table = table[:, :, None, 0]
    imag_table = table[:, :, None, 1]
    real_part = jnp.sum(real_table * sources[:, :, :, 0] - imag_table * sources[:, :, :, 1], axis=1)
    imag_part = jnp.sum(imag_table * sources[:, :, :, 0] + real_table * sources[:, :, :, 1], axis=1)
    return jnp.stack([real_part, imag_part], axis=2)


def disaggregate(incoming_rows, interp, cosine, sine_part, weights):
    parent_count = incoming_rows.shape[0]
    excite = incoming_rows.shape[1]
    widened = incoming_rows.astype(jnp.float32)[:, None]
    cosine_wide = cosine[None, :, None, :]
    sine_wide = sine_part[None, :, None, :]
    real_part = cosine_wide * widened[:, :, :, 0] + sine_wide * widened[:, :, :, 1]
    imag_part = cosine_wide * widened[:, :, :, 1] - sine_wide * widened[:, :, :, 0]
    shifted = jnp.stack([real_part, imag_part], axis=3).astype(jnp.bfloat16)
    leaf_in = jnp.dot(
        shifted.reshape(-1, interp.shape[1]), interp.T, preferred_element_type=jnp.float32
    ).astype(jnp.bfloat16)
    leaf_in = leaf_in.reshape(parent_count * 8 * excite, 2 * interp.shape[0])
    far_part = jnp.dot(leaf_in, weights.T, preferred_element_type=jnp.float32)
    return far_part.reshape(parent_count * 8, excite, weights.shape[0])


def select_cells(flat_field, cell_keys):
    cell_total = flat_field.shape[1]
    block_cells = math.gcd(cell_total, 1024)
    block_total = cell_total // block_cells
    positions = jnp.arange(block_cells, dtype=jnp.int32)

    def add_block(block_index, total):
        first = block_index * block_cells
        piece = lax.dynamic_slice_in_dim(flat_field, first, block_cells, 1)
        selector = (cell_keys[None, :] == (first + positions)[:, None]).astype(jnp.bfloat16)
        return total + jnp.dot(piece, selector, preferred_element_type=jnp.float32)

    empty = jnp.zeros((flat_field.shape[0], cell_keys.shape[0]), jnp.float32)
    return lax.fori_loop(0, block_total, add_block, empty)


def shards(
    volume_field,
    source,
    material,
    mat_real,
    mat_loss,
    surface_map,
    near_boxes,
    near_blocks,
    radiate,
    interp,
    phase_angle,
    far_parents,
    far_kind,
    translate,
):
    excite = volume_field.shape[1]
    cells_x = volume_field.shape[2]
    cells_y = volume_field.shape[3]
    cells_z = volume_field.shape[4]
    diagonal_coef = jnp.full(material.shape, 6.0, jnp.float32)
    loss_coef = jnp.zeros(material.shape, jnp.float32)
    for material_kind in range(mat_real.shape[0]):
        present = material == material_kind
        diagonal_coef = diagonal_coef + jnp.where(present, mat_real[material_kind], 0.0)
        loss_coef = loss_coef + jnp.where(present, mat_loss[material_kind], 0.0)
    channels = 2 * excite
    stacked = jnp.concatenate(
        [
            volume_field.reshape(channels, cells_x, cells_y, cells_z),
            source.reshape(channels, cells_x, cells_y, cells_z),
            diagonal_coef[None],
            loss_coef[None],
        ],
        axis=0,
    )
    widened = padded_2(stacked.astype(jnp.bfloat16), (("space", 1), ("shard", 2)), 2).astype(
        stacked.dtype
    )
    outer_field = widened[:channels].reshape(2, excite, cells_x + 4, cells_y + 4, cells_z)
    outer_source = widened[channels : 2 * channels, 1:-1, 1:-1].reshape(
        2, excite, cells_x + 2, cells_y + 2, cells_z
    )
    row_global = lax.axis_index("space") * cells_x - 1 + jnp.arange(cells_x + 2, dtype=jnp.int32)
    column_global = lax.axis_index("shard") * cells_y - 1 + jnp.arange(cells_y + 2, dtype=jnp.int32)
    row_inside = (row_global >= 0) & (row_global < cells_x * lax.axis_size("space"))
    column_inside = (column_global >= 0) & (column_global < cells_y * lax.axis_size("shard"))
    inside = row_inside[:, None, None] & column_inside[None, :, None]
    outer_diagonal = jnp.where(inside, widened[2 * channels, 1:-1, 1:-1], 1.0)
    outer_loss = widened[2 * channels + 1, 1:-1, 1:-1]
    first_sweep = relax_sweep(
        outer_field[:, :, 1:-1, 1:-1],
        neighbour_sum(outer_field),
        outer_source,
        outer_diagonal,
        outer_loss,
    )
    first_sweep = jnp.where(inside, first_sweep, 0.0)
    current = relax_sweep(
        first_sweep[:, :, 1:-1, 1:-1], neighbour_sum(first_sweep), source, diagonal_coef, loss_coef
    )
    box_count = surface_map.shape[0]
    unknowns = surface_map.shape[1]
    flat_field = current.reshape(2 * excite, cells_x * cells_y * cells_z).astype(jnp.bfloat16)
    sampled = select_cells(flat_field, surface_map.reshape(-1)).astype(jnp.bfloat16)
    sampled = sampled.reshape(2, excite, box_count, unknowns)
    currents = jnp.transpose(sampled, (2, 1, 0, 3)).reshape(box_count, excite, 2 * unknowns)
    device_rank = lax.axis_index("space") * lax.axis_size("shard") + lax.axis_index("shard")
    beside_all = padded_2(currents, (("shard", 0),), box_count)
    local_near = near_boxes - (device_rank * box_count - box_count)
    near_force = jnp.zeros((box_count, excite, 2 * unknowns), jnp.float32)
    for slot_index in range(near_boxes.shape[1]):
        picked = jnp.take(beside_all, local_near[:, slot_index], axis=0).reshape(
            box_count * excite, 2 * unknowns
        )
        near_force = near_force + jnp.dot(
            picked, near_blocks[slot_index], preferred_element_type=jnp.float32
        ).reshape(box_count, excite, 2 * unknowns)
    weights = block_matrix(radiate)
    leaf_dirs = interp.shape[0]
    leaf = jnp.dot(
        currents.reshape(box_count * excite, 2 * unknowns),
        weights,
        preferred_element_type=jnp.float32,
    ).astype(jnp.bfloat16)
    leaf = leaf.reshape(box_count, excite, 2, leaf_dirs)
    cosine = jnp.cos(phase_angle)
    sine_part = jnp.sin(phase_angle)
    parent_patterns = aggregate(leaf, interp, cosine, sine_part)
    directed = lax.all_to_all(parent_patterns, "shard", split_axis=3, concat_axis=0, tiled=True)
    group_parents = directed.shape[0]
    group_index = lax.axis_index("space")
    target_ids = lax.dynamic_slice_in_dim(
        far_parents, group_index * group_parents, group_parents, 0
    )
    target_kinds = lax.dynamic_slice_in_dim(far_kind, group_index * group_parents, group_parents, 0)
    table = jnp.take(translate, target_kinds, axis=0)
    gathered = lax.all_gather(directed, "space", axis=0, tiled=True)
    sources = jnp.take(gathered, target_ids, axis=0).astype(jnp.float32)
    incoming = combine_far(sources, table).astype(jnp.bfloat16)
    far_force = disaggregate(
        lax.all_to_all(incoming, "shard", split_axis=0, concat_axis=3, tiled=True),
        interp,
        cosine,
        sine_part,
        weights,
    )
    forcing = near_force + far_force
    return (current, forcing)


def solution(mesh):
    return jax.shard_map(
        shards,
        mesh=mesh,
        in_specs=(
            P(None, None, "space", "shard", None),
            P(None, None, "space", "shard", None),
            P("space", "shard", None),
            P(),
            P(),
            P(("space", "shard"), None),
            P(("space", "shard"), None),
            P(),
            P(),
            P(),
            P(),
            P(),
            P(),
            P(None, None, "shard"),
        ),
        out_specs=(P(None, None, "space", "shard", None), P(("space", "shard"), None, None)),
        check_vma=False,
    )
```

profile of v0, /device:TPU:0, one launch (start us, length us, event | category | flops | bytes accessed | tf_op | source)
XLA Modules:
  0.0 182.6 jit_solution(5220939384639286865)
XLA Ops:
  11.9 5.7 %convert_bitcast_fusion.7 = (bf16[1,4,16,128]{3,2,1,0:T(8,128)(2,1)S(1)}, f32[4,16,128]{2,1,0:T(8,128)}, pred[4,16,128]{2,1,0:T(8,128)(4,1)S(1)}, pred[4,16,128]...) fusion(f32[]{:T(128)} %bitcast.9, f32[]{:T(128)} %bitcast.8, ...), kind=kLoop, calls=%fused_computation.120 | loop fusion | flops 204800 | bytes 147488 | tf_op jit(solution)/shard_map/broadcast_in_dim | solution.py:132
  17.6 5.6 %convert_bitcast_fusion.6 = (bf16[1,4,16,128]{3,2,1,0:T(8,128)(2,1)S(1)}, f32[4,16,128]{2,1,0:T(8,128)}) fusion(pred[4,16,128]{2,1,0:T(8,128)(4,1)S(1)} %get-tuple-element.150, f32[]{:T(128)} %bitcast.18, pred[4,16,128]{2,1,0:T(8,128)(4,1)S(1)} %get-tuple-element.149, f32[]{:T(128)} %bitcast.17, pred[4,16,128]{2,1,0:T(8,128)(4,1)S(1)} %get-tuple-element.148, ...), kind=kLoop, calls=%fused_computation.119 | loop fusion | flops 131072 | bytes 114720 | tf_op jit(solution)/shard_map/broadcast_in_dim | solution.py:133
  24.6 3.2 %collective-permute-start = (bf16[66,2,16,128]{3,2,1,0:T(8,128)(2,1)}, bf16[66,2,16,128]{3,2,1,0:T(8,128)(2,1)}, u32[]{:S(2)}, u32[]{:S(2)}) collective-permute-start(bf16[66,2,16,128]{3,2,1,0:T(8,128)(2,1)} %get-tuple-element.165), channel_id=1, source_target_pairs={{0,8},{8,16},{16,24},{1,9},{9,17},{17,25},{2,10},{10,18},{18,26},{... | collective-permute-start | bytes 1622024 | tf_op jit(solution)/shard_map/ppermute | solution.py:17
  30.9 2.4 %collective-permute-done.1 = bf16[66,2,16,128]{3,2,1,0:T(8,128)(2,1)} collective-permute-done((bf16[66,2,16,128]{3,2,1,0:T(8,128)(2,1)}, bf16[66,2,16,128]{3,2,1,0:T(8,128)(2,1)}, u32[]{:S(2)}, u32[]{:S(2)}) %collective-permute-start.1) | collective-permute-done | bytes 540704 | tf_op jit(solution)/shard_map/ppermute | solution.py:18
  33.3 4.5 %pad_maximum_fusion.7 = (bf16[66,8,2,128]{3,2,1,0:T(2,128)(2,1)}, bf16[66,8,2,128]{3,2,1,0:T(2,128)(2,1)}) fusion(bf16[66,2,16,128]{3,2,1,0:T(8,128)(2,1)} %collective-permute-done.1, bf16[66,2,16,128]{3,2,1,0:T(8,128)(2,1)} %collective-permute-done, bf16[1,4,16,128]{3,2,1,0:T(8,128)(2,1)} %copy-done.11, bf16[1,4,16,128]{3,2,1,0:T(8,128)(2,1)S(1)} %get-tuple-element.141, ...), kind=kLoop, calls=%fused_computation.74 | loop fusion | flops 3244032 | bytes 2703360 | tf_op jit(solution)/shard_map/slice | solution.py:15
  37.8 4.1 %collective-permute-start.2 = (bf16[66,8,2,128]{3,2,1,0:T(2,128)(2,1)}, bf16[66,8,2,128]{3,2,1,0:T(2,128)(2,1)}, u32[]{:S(2)}, u32[]{:S(2)}) collective-permute-start(bf16[66,8,2,128]{3,2,1,0:T(2,128)(2,1)} %get-tuple-element.163), channel_id=1, source_target_pairs={{0,1},{1,2},{2,3},{3,4},{4,5},{5,6},{6,7},{8,9},{9,10},{10,11},{11... | collective-permute-start | bytes 811016 | tf_op jit(solution)/shard_map/ppermute | solution.py:17
  45.5 5.1 %collective-permute-done.3 = bf16[66,8,2,128]{3,2,1,0:T(2,128)(2,1)} collective-permute-done((bf16[66,8,2,128]{3,2,1,0:T(2,128)(2,1)}, bf16[66,8,2,128]{3,2,1,0:T(2,128)(2,1)}, u32[]{:S(2)}, u32[]{:S(2)}) %collective-permute-start.3) | collective-permute-done | bytes 270368 | tf_op jit(solution)/shard_map/ppermute | solution.py:18
  50.6 7.1 %maximum_convert_fusion = f32[66,8,20,128]{3,2,1,0:T(8,128)S(1)} fusion(bf16[66,8,2,128]{3,2,1,0:T(2,128)(2,1)} %collective-permute-done.3, bf16[66,2,16,128]{3,2,1,0:T(8,128)(2,1)} %collective-permute-done.1, bf16[1,4,16,128]{3,2,1,0:T(8,128)(2,1)} %copy-done.11, bf16[1,4,16,128]{3,2,1,0:T(8,128)(2,1)S(1)} %get-tuple-element.141, ...), kind=kLoop, calls=%fused_computation.15 | loop fusion | flops 21626880 | bytes 8110080 | tf_op jit(solution)/shard_map/convert_element_type | solution.py:137
  65.3 12.8 %while.14 = (s32[]{:T(128)}, f32[32,2048]{1,0:T(8,128)S(1)}, bf16[32,8192]{1,0:T(8,128)(2,1)S(1)}, s32[16,128]{1,0:T(8,128)S(1)}, s32[]{:T(128)}, /*index=5*/s32[]{:T(128)}, s32[]{:T(128)}, s32[]{:T(128)}) while((s32[]{:T(128)}, f32[32,2048]{1,0:T(8,128)S(1)}, bf16[32,8192]{1,0:T(8,128)(2,1)S(1)}, s32[16,128]{1,0:T(8,128)S(1)}, ...), condition=%wide.region_1.2_spmd.clone, body=%wide.region_0.1_spmd.clone.sunk | while | flops 136446976 | bytes 606365 | solution.py:98
  81.0 3.7 %copy.57 = bf16[2,16,2,2048]{1,2,0,3:T(2,128)(2,1)} copy(bf16[2,16,2,2048]{3,1,0,2:T(8,128)(2,1)S(1)} %pad_maximum_fusion.8) | data formatting | bytes 524288 | tf_op jit(solution)/shard_map/stack | solution.py:57
  84.7 4.0 %reshape.250 = bf16[8,2,8192]{2,1,0:T(2,128)(2,1)} reshape(bf16[2048,2,2,16]{3,2,1,0:T(2,128)(2,1)} %bitcast.164) | data formatting | bytes 524288
  88.8 5.2 %all-to-all-start = ((bf16[8,2,8192]{2,1,0:T(2,128)(2,1)}), bf16[8,2,8192]{2,1,0:T(2,128)(2,1)S(1)}, u32[]{:S(2)}, u32[]{:S(2)}) async-start(bf16[8,2,8192]{2,1,0:T(2,128)(2,1)} %reshape.250), calls=%async_computation | async-start | bytes 524288 | tf_op jit(solution)/shard_map/all_to_all | solution.py:190
  97.1 5.1 %all-to-all-done = bf16[8,2,8192]{2,1,0:T(2,128)(2,1)S(1)} async-done(((bf16[8,2,8192]{2,1,0:T(2,128)(2,1)}), bf16[8,2,8192]{2,1,0:T(2,128)(2,1)S(1)}, u32[]{:S(2)}, u32[]{:S(2)}) %all-to-all-start) | async-done | bytes 262176 | tf_op jit(solution)/shard_map/all_to_all | solution.py:190
  102.2 2.4 %reshape.251 = bf16[2048,2,2,16]{3,2,1,0:T(2,128)(2,1)} reshape(bf16[8,2,8192]{2,1,0:T(2,128)(2,1)S(1)} %all-to-all-done) | data formatting | bytes 524288
  104.5 5.6 %copy.65 = bf16[2,16,2,8,256]{4,1,2,0,3:T(8,128)(2,1)} copy(bf16[2,16,2,8,256]{1,2,0,4,3:T(2,128)(2,1)} %bitcast.165) | data formatting | bytes 524288 | tf_op jit(solution)/shard_map/all_to_all | solution.py:190
  117.3 5.5 %collective-permute-done.5 = bf16[16,16,256]{2,1,0:T(8,128)(2,1)S(1)} collective-permute-done((bf16[16,16,256]{2,1,0:T(8,128)(2,1)S(1)}, bf16[16,16,256]{2,1,0:T(8,128)(2,1)S(1)}, u32[]{:S(2)}, u32[]{:S(2)}) %collective-permute-start.5) | collective-permute-done | bytes 131104 | tf_op jit(solution)/shard_map/ppermute | solution.py:18
  130.8 3.2 %gather_fusion.1 = bf16[128,16,2,256]{3,1,2,0:T(8,128)(2,1)} fusion(bf16[64,16,2,256]{3,1,2,0:T(8,128)(2,1)} %all-gather.2.cloned.1.call-done, s32[1024]{0:T(1024)S(1)} %pad_clamp_fusion), kind=kCustom, calls=%fused_computation.5 | custom fusion | bytes 4194816 | tf_op jit(solution)/shard_map/jit(_take)/gather | solution.py:199
  137.6 5.5 %all-to-all-start.1 = ((bf16[16,16,2,256]{3,1,2,0:T(8,128)(2,1)}), bf16[16,16,2,256]{3,1,2,0:T(8,128)(2,1)S(1)}, u32[]{:S(2)}, u32[]{:S(2)}) async-start(bf16[16,16,2,256]{3,1,2,0:T(8,128)(2,1)} %pad_maximum_fusion.9), calls=%async_computation.1 | async-start | bytes 524288 | tf_op jit(solution)/shard_map/all_to_all | solution.py:202
  145.9 6.5 %all-to-all-done.1 = bf16[16,16,2,256]{3,1,2,0:T(8,128)(2,1)S(1)} async-done(((bf16[16,16,2,256]{3,1,2,0:T(8,128)(2,1)}), bf16[16,16,2,256]{3,1,2,0:T(8,128)(2,1)S(1)}, u32[]{:S(2)}, u32[]{:S(2)}) %all-to-all-start.1) | async-done | bytes 262176 | tf_op jit(solution)/shard_map/all_to_all | solution.py:202
  152.9 4.4 %add_convert_fusion = (bf16[2,8,16,1,2048]{4,3,2,1,0:T(2,128)(2,1)S(1)}, bf16[2,8,16,1,2048]{4,3,2,1,0:T(2,128)(2,1)S(1)}) fusion(f32[2,16,2048]{2,1,0:T(8,128)S(1)} %get-tuple-element.170, f32[8,2048]{1,0:T(8,128)S(1)} %get-tuple-element.178, f32[2,16,2048]{2,1,0:T(8,128)S(1)} %get-tuple-element.169, f32[8,2048]{1,0:T(8,128)S(1)} %get-tuple-element.177), kind=kLoop, calls=%fused_computation.34 | loop fusion | flops 4194304 | bytes 2752512 | tf_op jit(solution)/shard_map/convert.3
  157.3 5.2 %pad_maximum_fusion = bf16[2,8,16,2,2048]{4,3,2,1,0:T(2,128)(2,1)} fusion(bf16[2,8,16,1,2048]{4,3,2,1,0:T(2,128)(2,1)S(1)} %get-tuple-element.168, bf16[2,8,16,1,2048]{4,3,2,1,0:T(2,128)(2,1)S(1)} %get-tuple-element.167), kind=kLoop, calls=%fused_computation.30 | loop fusion | flops 4194304 | bytes 4194304 | tf_op jit(solution)/shard_map/stack | solution.py:76
  162.5 4.1 %convert_element_type.61 = bf16[512,2048]{1,0:T(8,128)(2,1)} reshape(bf16[2,8,16,2,2048]{4,3,2,1,0:T(2,128)(2,1)} %pad_maximum_fusion) | data formatting | bytes 4194304 | tf_op jit(solution)/shard_map/convert_element_type | solution.py:76
  166.6 3.7 %convolution_convert_fusion = bf16[512,512]{1,0:T(8,128)(2,1)} fusion(bf16[512,2048]{1,0:T(8,128)(2,1)} %convert_element_type.61, bf16[512,2048]{1,0:T(8,128)(2,1)S(1)} %copy-done), kind=kOutput, calls=%fused_computation.40 | convolution fusion | flops 1074003968 | bytes 4718592 | tf_op jit(solution)/shard_map/dot_general | solution.py:77
  170.3 2.1 %dot_general.43 = bf16[16,16,1024]{2,1,0:T(8,128)(2,1)} reshape(bf16[512,512]{1,0:T(8,128)(2,1)} %convolution_convert_fusion) | data formatting | bytes 1048576 | tf_op jit(solution)/shard_map/dot_general | solution.py:81
  (154 shorter events, 63.7 us)
Async XLA Ops:
  7.2 71.9 %copy-start = (bf16[512,2048]{1,0:T(8,128)(2,1)S(1)}, bf16[512,2048]{1,0:T(8,128)(2,1)}, u32[]{:S(2)}) copy-start(bf16[512,2048]{1,0:T(8,128)(2,1)} %param.27) | copy-start | bytes 6291460
  23.2 5.9 %copy-start.5 = (bf16[2,128,512]{2,1,0:T(8,128)(2,1)S(1)}, bf16[2,128,512]{2,1,0:T(8,128)(2,1)}, u32[]{:S(2)}) copy-start(bf16[2,128,512]{2,1,0:T(8,128)(2,1)} %param.26) | copy-start | bytes 786436
  24.6 6.3 %collective-permute-start = (bf16[66,2,16,128]{3,2,1,0:T(8,128)(2,1)}, bf16[66,2,16,128]{3,2,1,0:T(8,128)(2,1)}, u32[]{:S(2)}, u32[]{:S(2)}) collective-permute-start(bf16[66,2,16,128]{3,2,1,0:T(8,128)(2,1)} %get-tuple-element.165), channel_id=1, source_target_pairs={{0,8},{8,16},{16,24},{1,9},{9,17},{17,25},{2,10},{10,18},{18,26},{... | collective-permute-start | bytes 1622024 | tf_op jit(solution)/shard_map/ppermute | solution.py:17
  27.8 5.5 %collective-permute-start.1 = (bf16[66,2,16,128]{3,2,1,0:T(8,128)(2,1)}, bf16[66,2,16,128]{3,2,1,0:T(8,128)(2,1)}, u32[]{:S(2)}, u32[]{:S(2)}) collective-permute-start(bf16[66,2,16,128]{3,2,1,0:T(8,128)(2,1)} %get-tuple-element.166), channel_id=1, source_target_pairs={{8,0},{16,8},{24,16},{9,1},{17,9},{25,17},{10,2},{18,10},{26,18},{... | collective-permute-start | bytes 1622024 | tf_op jit(solution)/shard_map/ppermute | solution.py:18
  37.8 7.7 %collective-permute-start.2 = (bf16[66,8,2,128]{3,2,1,0:T(2,128)(2,1)}, bf16[66,8,2,128]{3,2,1,0:T(2,128)(2,1)}, u32[]{:S(2)}, u32[]{:S(2)}) collective-permute-start(bf16[66,8,2,128]{3,2,1,0:T(2,128)(2,1)} %get-tuple-element.163), channel_id=1, source_target_pairs={{0,1},{1,2},{2,3},{3,4},{4,5},{5,6},{6,7},{8,9},{9,10},{10,11},{11... | collective-permute-start | bytes 811016 | tf_op jit(solution)/shard_map/ppermute | solution.py:17
  41.9 8.7 %collective-permute-start.3 = (bf16[66,8,2,128]{3,2,1,0:T(2,128)(2,1)}, bf16[66,8,2,128]{3,2,1,0:T(2,128)(2,1)}, u32[]{:S(2)}, u32[]{:S(2)}) collective-permute-start(bf16[66,8,2,128]{3,2,1,0:T(2,128)(2,1)} %get-tuple-element.164), channel_id=1, source_target_pairs={{1,0},{2,1},{3,2},{4,3},{5,4},{6,5},{7,6},{9,8},{10,9},{11,10},{12... | collective-permute-start | bytes 811016 | tf_op jit(solution)/shard_map/ppermute | solution.py:18
  44.7 12.9 %copy-start.20 = (pred[6,18]{1,0:T(8,128)(4,1)S(1)}, pred[6,18]{1,0:T(8,128)(4,1)}, u32[]{:S(2)}) copy-start(pred[6,18]{1,0:T(8,128)(4,1)} %broadcast_and_fusion) | copy-start | bytes 328
  65.3 13.1 %copy-start.14 = (bf16[128,512]{1,0:T(8,128)(2,1)S(1)}, bf16[128,512]{1,0:T(8,128)(2,1)}, u32[]{:S(2)}) copy-start(bf16[128,512]{1,0:T(8,128)(2,1)} %fusion.63) | copy-start | bytes 393220
  65.3 13.1 %copy-start.16 = (bf16[128,512]{1,0:T(8,128)(2,1)S(1)}, bf16[128,512]{1,0:T(8,128)(2,1)}, u32[]{:S(2)}) copy-start(bf16[128,512]{1,0:T(8,128)(2,1)} %get-tuple-element.173) | copy-start | bytes 393220
  65.3 13.1 %copy-start.18 = (bf16[128,512]{1,0:T(8,128)(2,1)S(1)}, bf16[128,512]{1,0:T(8,128)(2,1)}, u32[]{:S(2)}) copy-start(bf16[128,512]{1,0:T(8,128)(2,1)} %get-tuple-element.174) | copy-start | bytes 393220
  81.0 13.0 %copy-start.21 = (s32[64,8]{0,1:T(8,128)S(1)}, s32[64,8]{0,1:T(8,128)}, u32[]{:S(2)}) copy-start(s32[64,8]{0,1:T(8,128)} %param.29) | copy-start | bytes 6148
  81.0 13.0 %copy-start.22 = (s32[64,8]{0,1:T(8,128)S(1)}, s32[64,8]{0,1:T(8,128)}, u32[]{:S(2)}) copy-start(s32[64,8]{0,1:T(8,128)} %param.30) | copy-start | bytes 6148
  84.7 12.4 %copy-start.26 = (s32[16,4]{0,1:T(4,128)S(1)}, s32[16,4]{0,1:T(4,128)}, u32[]{:S(2)}) copy-start(s32[16,4]{0,1:T(4,128)} %param.24) | copy-start | bytes 772
  88.8 13.4 %all-to-all-start = ((bf16[8,2,8192]{2,1,0:T(2,128)(2,1)}), bf16[8,2,8192]{2,1,0:T(2,128)(2,1)S(1)}, u32[]{:S(2)}, u32[]{:S(2)}) async-start(bf16[8,2,8192]{2,1,0:T(2,128)(2,1)} %reshape.250), calls=%async_computation | async-start | bytes 524288 | tf_op jit(solution)/shard_map/all_to_all | solution.py:190
  93.9 36.9 %all-gather.2.cloned.1.call-start = ((), (), s32[]{:S(2)}) async-start(), calls=%async_computation.2 | async-start | bytes 1310720 | tf_op jit(solution)/shard_map/all_gather | solution.py:198
  110.2 17.7 %copy-start.6 = (bf16[4,256,256]{2,1,0:T(8,128)(2,1)S(1)}, bf16[4,256,256]{2,1,0:T(8,128)(2,1)}, u32[]{:S(2)}) copy-start(bf16[4,256,256]{2,1,0:T(8,128)(2,1)} %param.25) | copy-start | bytes 1572868
  111.3 5.9 %collective-permute-start.4 = (bf16[16,16,256]{2,1,0:T(8,128)(2,1)S(1)}, bf16[16,16,256]{2,1,0:T(8,128)(2,1)S(1)}, u32[]{:S(2)}, u32[]{:S(2)}) collective-permute-start(bf16[16,16,256]{2,1,0:T(8,128)(2,1)S(1)} %reshape.177), channel_id=1, source_target_pairs={{0,1},{1,2},{2,3},{3,4},{4,5},{5,6},{6,7},{8,9},{9,10},{10,11},{11... | collective-permute-start | bytes 393224 | tf_op jit(solution)/shard_map/ppermute | solution.py:17
  115.9 6.8 %collective-permute-start.5 = (bf16[16,16,256]{2,1,0:T(8,128)(2,1)S(1)}, bf16[16,16,256]{2,1,0:T(8,128)(2,1)S(1)}, u32[]{:S(2)}, u32[]{:S(2)}) collective-permute-start(bf16[16,16,256]{2,1,0:T(8,128)(2,1)S(1)} %reshape.177), channel_id=1, source_target_pairs={{1,0},{2,1},{3,2},{4,3},{5,4},{6,5},{7,6},{9,8},{10,9},{11,10},{12... | collective-permute-start | bytes 393224 | tf_op jit(solution)/shard_map/ppermute | solution.py:18
  136.0 7.1 %copy-start.25 = (pred[16]{0:T(512)(128)(4,1)S(1)}, pred[16]{0:T(512)(128)(4,1)}, u32[]{:S(2)}) copy-start(pred[16]{0:T(512)(128)(4,1)} %get-tuple-element.181) | copy-start | bytes 52
  136.0 8.9 %copy-start.9 = (bf16[16,16,256]{2,1,0:T(8,128)(2,1)S(1)}, bf16[16,16,256]{2,1,0:T(8,128)(2,1)}, u32[]{:S(2)}) copy-start(bf16[16,16,256]{2,1,0:T(8,128)(2,1)} %gather_fusion.5) | copy-start | bytes 393220
  136.1 8.9 %copy-start.24 = (pred[16]{0:T(512)(128)(4,1)S(1)}, pred[16]{0:T(512)(128)(4,1)}, u32[]{:S(2)}) copy-start(pred[16]{0:T(512)(128)(4,1)} %get-tuple-element.179) | copy-start | bytes 52
  137.6 14.8 %all-to-all-start.1 = ((bf16[16,16,2,256]{3,1,2,0:T(8,128)(2,1)}), bf16[16,16,2,256]{3,1,2,0:T(8,128)(2,1)S(1)}, u32[]{:S(2)}, u32[]{:S(2)}) async-start(bf16[16,16,2,256]{3,1,2,0:T(8,128)(2,1)} %pad_maximum_fusion.9), calls=%async_computation.1 | async-start | bytes 524288 | tf_op jit(solution)/shard_map/all_to_all | solution.py:202
  166.6 5.8 %copy-start.15 = (bf16[128,512]{1,0:T(8,128)(2,1)S(1)}, bf16[128,512]{1,0:T(8,128)(2,1)}, u32[]{:S(2)}) copy-start(bf16[128,512]{1,0:T(8,128)(2,1)} %fusion.63) | copy-start | bytes 393220
  166.6 5.8 %copy-start.17 = (bf16[128,512]{1,0:T(8,128)(2,1)S(1)}, bf16[128,512]{1,0:T(8,128)(2,1)}, u32[]{:S(2)}) copy-start(bf16[128,512]{1,0:T(8,128)(2,1)} %get-tuple-element.173) | copy-start | bytes 393220
  (13 other events, 32.7 us)
Sparse Core Ops, SparseCore 0:
  110.3 20.4 all-gather.1
where the time goes:
time: 184 us; the launch traced here: 183 us
  other arithmetic  46.8 us (25%)
  local copies, waits for them, and re-layouts  44.7 us (24%)
  waiting for transfers between devices  27.1 us (15%)
  matrix products  25 us (14%)
  starting transfers between devices  23.9 us (13%)
  between operations  14.7 us (8%)
    ppermute x3, waiting for transfers between devices, padded_2(): after = lax.ppermute(leading, axis, down)  13 us
    dot_general x8, matrix products, add_block(): return total + jnp.dot(piece, selector, preferred_element_type=jnp.float32)  12.5 us
    ppermute x3, starting transfers between devices, padded_2(): before = lax.ppermute(last, axis, up)  9.22 us
    unnamed x63, local copies, waits for them, and re-layouts  8.24 us
    convert_element_type x1, other arithmetic, shards(): padded_2(stacked.astype(jnp.bfloat16), (('space', 1), ('shard', 2)), 2)  7.05 us
    all_to_all x1, waiting for transfers between devices, shards(): lax.all_to_all(incoming, 'shard', split_axis=0, concat_axis=3, tiled=True)  6.52 us
    another operation x3, other arithmetic  5.8 us
    dot_general x4, matrix products, shards(): jnp.dot(picked, near_blocks[slot_index], preferred_element_type=jnp.float32)  5.76 us
  transfers between devices with their start and end apart: 9, of which 7 were waited for; matrix products, arithmetic and copies ran while one was open for 10% of the time, Pallas kernels for 0%

commit v1 on v0

--- a/solution.py
+++ b/solution.py
@@ -187,7 +187,19 @@
     cosine = jnp.cos(phase_angle)
     sine_part = jnp.sin(phase_angle)
     parent_patterns = aggregate(leaf, interp, cosine, sine_part)
-    directed = lax.all_to_all(parent_patterns, "shard", split_axis=3, concat_axis=0, tiled=True)
+    ways, here = (lax.axis_size("shard"), lax.axis_index("shard"))
+    width_2 = parent_patterns.shape[3] // ways
+    dims = list(parent_patterns.shape)
+    dims[3] = width_2
+    height = dims[0]
+    dims[0] = height * ways
+    full = jnp.zeros(dims, parent_patterns.dtype)
+    for mask in range(ways):
+        part = lax.dynamic_slice_in_dim(parent_patterns, (here ^ mask) * width_2, width_2, axis=3)
+        if mask:
+            part = lax.ppermute(part, "shard", [(d, d ^ mask) for d in range(ways)])
+        full = lax.dynamic_update_slice_in_dim(full, part, (here ^ mask) * height, axis=0)
+    directed = full
     group_parents = directed.shape[0]
     group_index = lax.axis_index("space")
     target_ids = lax.dynamic_slice_in_dim(

time: 184 us -> 187 us (1.016)
  local copies, waits for them, and re-layouts: 44.7 us -> 30.5 us
  matrix products: 25 us -> 38.1 us
  starting transfers between devices: 23.9 us -> 33 us
  waiting for transfers between devices: 27.1 us -> 22.8 us
    ppermute x0 -> x7, starting transfers between devices: none -> 12.9 us  [shards(): part = lax.ppermute(part, 'shard', [(d, d ^ mask) for d in range(ways)])]
    dot_general x8, matrix products: 12.5 us -> 24.7 us  [add_block(): return total + jnp.dot(piece, selector, preferred_element_type=jnp.float32)]
    ppermute x3, waiting for transfers between devices: 13 us -> 6.3 us  [padded_2(): after = lax.ppermute(leading, axis, down)]
    unnamed x63, local copies, waits for them, and re-layouts: 8.24 us -> 2.49 us
    all_to_all x1 -> x0, local copies, waits for them, and re-layouts: 5.63 us -> none  [shards(): lax.all_to_all(parent_patterns, 'shard', split_axis=3, concat_axis=0, til...]
    all_to_all x1 -> x0, starting transfers between devices: 5.16 us -> none  [shards(): lax.all_to_all(parent_patterns, 'shard', split_axis=3, concat_axis=0, til...]
    all_to_all x1 -> x0, waiting for transfers between devices: 5.06 us -> none  [shards(): lax.all_to_all(parent_patterns, 'shard', split_axis=3, concat_axis=0, til...]
    ppermute x0 -> x7, waiting for transfers between devices: none -> 4.54 us  [shards(): part = lax.ppermute(part, 'shard', [(d, d ^ mask) for d in range(ways)])]
  transfers between devices with their start and end apart: 9 -> 15, of which waited for: 7 -> 9; matrix products, arithmetic and copies ran while one was open for 10% -> 10% of each run, Pallas kernels for 0% -> 0%
where the time goes in v1:
time: 187 us; the launch traced here: 186 us
  other arithmetic  47 us (25%)
  matrix products  38.1 us (20%)
  starting transfers between devices  33 us (18%)
  local copies, waits for them, and re-layouts  30.5 us (16%)
  waiting for transfers between devices  22.8 us (12%)
  between operations  14.8 us (8%)
    dot_general x8, matrix products, add_block(): return total + jnp.dot(piece, selector, preferred_element_type=jnp.float32)  24.7 us
    ppermute x7, starting transfers between devices, shards(): part = lax.ppermute(part, 'shard', [(d, d ^ mask) for d in range(ways)])  12.9 us
    ppermute x3, starting transfers between devices, padded_2(): before = lax.ppermute(last, axis, up)  10.6 us
    convert_element_type x1, other arithmetic, shards(): padded_2(stacked.astype(jnp.bfloat16), (('space', 1), ('shard', 2)), 2)  7.05 us
    dot_general x4, matrix products, shards(): jnp.dot(picked, near_blocks[slot_index], preferred_element_type=jnp.float32)  6.67 us
    ppermute x3, waiting for transfers between devices, padded_2(): after = lax.ppermute(leading, axis, down)  6.3 us
    another operation x3, other arithmetic  5.8 us
    broadcast_in_dim x1, other arithmetic, shards(): diagonal_coef[None]  5.68 us
  transfers between devices with their start and end apart: 15, of which 9 were waited for; matrix products, arithmetic and copies ran while one was open for 10% of the time, Pallas kernels for 0%

profile of v1, /device:TPU:0, one launch (start us, length us, event | category | flops | bytes accessed | tf_op | source)
XLA Modules:
  0.0 186.2 jit_solution(2825481755675530046)
XLA Ops:
  11.9 5.7 %convert_bitcast_fusion.7 = (bf16[1,4,16,128]{3,2,1,0:T(8,128)(2,1)S(1)}, f32[4,16,128]{2,1,0:T(8,128)}, pred[4,16,128]{2,1,0:T(8,128)(4,1)S(1)}, pred[4,16,128]...) fusion(f32[]{:T(128)} %bitcast.9, f32[]{:T(128)} %bitcast.8, ...), kind=kLoop, calls=%fused_computation.151 | loop fusion | flops 204800 | bytes 147488 | tf_op jit(solution)/shard_map/broadcast_in_dim | solution.py:132
  17.6 5.6 %convert_bitcast_fusion.6 = (bf16[1,4,16,128]{3,2,1,0:T(8,128)(2,1)S(1)}, f32[4,16,128]{2,1,0:T(8,128)}) fusion(pred[4,16,128]{2,1,0:T(8,128)(4,1)S(1)} %get-tuple-element.150, f32[]{:T(128)} %bitcast.18, pred[4,16,128]{2,1,0:T(8,128)(4,1)S(1)} %get-tuple-element.149, f32[]{:T(128)} %bitcast.17, pred[4,16,128]{2,1,0:T(8,128)(4,1)S(1)} %get-tuple-element.148, ...), kind=kLoop, calls=%fused_computation.150 | loop fusion | flops 131072 | bytes 114720 | tf_op jit(solution)/shard_map/broadcast_in_dim | solution.py:133
  24.6 3.2 %collective-permute-start = (bf16[66,2,16,128]{3,2,1,0:T(8,128)(2,1)}, bf16[66,2,16,128]{3,2,1,0:T(8,128)(2,1)}, u32[]{:S(2)}, u32[]{:S(2)}) collective-permute-start(bf16[66,2,16,128]{3,2,1,0:T(8,128)(2,1)} %get-tuple-element.165), channel_id=1, source_target_pairs={{0,8},{8,16},{16,24},{1,9},{9,17},{17,25},{2,10},{10,18},{18,26},{... | collective-permute-start | bytes 1622024 | tf_op jit(solution)/shard_map/ppermute | solution.py:17
  33.3 4.5 %pad_maximum_fusion.7 = (bf16[66,8,2,128]{3,2,1,0:T(2,128)(2,1)}, bf16[66,8,2,128]{3,2,1,0:T(2,128)(2,1)}) fusion(bf16[66,2,16,128]{3,2,1,0:T(8,128)(2,1)} %collective-permute-done.1, bf16[66,2,16,128]{3,2,1,0:T(8,128)(2,1)} %collective-permute-done, bf16[1,4,16,128]{3,2,1,0:T(8,128)(2,1)} %copy-done.12, bf16[1,4,16,128]{3,2,1,0:T(8,128)(2,1)S(1)} %get-tuple-element.141, ...), kind=kLoop, calls=%fused_computation.90 | loop fusion | flops 3244032 | bytes 2703360 | tf_op jit(solution)/shard_map/slice | solution.py:15
  37.8 4.6 %collective-permute-start.2 = (bf16[66,8,2,128]{3,2,1,0:T(2,128)(2,1)}, bf16[66,8,2,128]{3,2,1,0:T(2,128)(2,1)}, u32[]{:S(2)}, u32[]{:S(2)}) collective-permute-start(bf16[66,8,2,128]{3,2,1,0:T(2,128)(2,1)} %get-tuple-element.163), channel_id=1, source_target_pairs={{0,1},{1,2},{2,3},{3,4},{4,5},{5,6},{6,7},{8,9},{9,10},{10,11},{11... | collective-permute-start | bytes 811016 | tf_op jit(solution)/shard_map/ppermute | solution.py:17
  51.0 7.1 %maximum_convert_fusion = f32[66,8,20,128]{3,2,1,0:T(8,128)S(1)} fusion(bf16[66,8,2,128]{3,2,1,0:T(2,128)(2,1)} %collective-permute-done.3, bf16[66,2,16,128]{3,2,1,0:T(8,128)(2,1)} %collective-permute-done.1, bf16[1,4,16,128]{3,2,1,0:T(8,128)(2,1)} %copy-done.12, bf16[1,4,16,128]{3,2,1,0:T(8,128)(2,1)S(1)} %get-tuple-element.141, ...), kind=kLoop, calls=%fused_computation.15 | loop fusion | flops 21626880 | bytes 8110080 | tf_op jit(solution)/shard_map/convert_element_type | solution.py:137
  65.8 24.8 %while.14 = (s32[]{:T(128)}, f32[32,2048]{1,0:T(8,128)}, bf16[32,8192]{1,0:T(8,128)(2,1)S(1)}, s32[16,128]{1,0:T(8,128)S(1)}, s32[]{:T(128)}, /*index=5*/s32[]{:T(128)}, s32[]{:T(128)}, s32[]{:T(128)}) while((s32[]{:T(128)}, f32[32,2048]{1,0:T(8,128)}, bf16[32,8192]{1,0:T(8,128)(2,1)S(1)}, s32[16,128]{1,0:T(8,128)S(1)}, s32[]{:T(128)}, ...), condition=%wide.region_1.2_spmd.clone, body=%wide.region_0.1_spmd.clone.sunk | while | flops 136446976 | bytes 606365 | solution.py:98
  68.1 3.2 %fusion.88 = f32[32,2048]{1,0:T(8,128)} fusion(s32[2048]{0:T(1024)S(1)} %bitcast.177, s32[1024]{0:T(1024)S(1)} %iota_add_fusion.2, f32[32,2048]{1,0:T(8,128)} %get-tuple-element.249, pred[]{:T(512)S(6)} %compare.7, bf16[32,8192]{1,0:T(8,128)(2,1)S(1)} %get-tuple-element.258, s32[]{:T(128)S(6)} %select_n.260), kind=kOutput, calls=%fused_computation.11.clone.1 | convolution fusion | flops 136445952 | bytes 602117 | tf_op jit(solution)/shard_map/while/body/eval_jaxpr/dot_general | solution.py:95
  71.3 3.2 %fusion.88 = f32[32,2048]{1,0:T(8,128)} fusion(s32[2048]{0:T(1024)S(1)} %bitcast.177, s32[1024]{0:T(1024)S(1)} %iota_add_fusion.2, f32[32,2048]{1,0:T(8,128)} %get-tuple-element.249, pred[]{:T(512)S(6)} %compare.7, bf16[32,8192]{1,0:T(8,128)(2,1)S(1)} %get-tuple-element.258, s32[]{:T(128)S(6)} %select_n.260), kind=kOutput, calls=%fused_computation.11.clone.1 | convolution fusion | flops 136445952 | bytes 602117 | tf_op jit(solution)/shard_map/while/body/eval_jaxpr/dot_general | solution.py:95
  74.5 3.2 %fusion.88 = f32[32,2048]{1,0:T(8,128)} fusion(s32[2048]{0:T(1024)S(1)} %bitcast.177, s32[1024]{0:T(1024)S(1)} %iota_add_fusion.2, f32[32,2048]{1,0:T(8,128)} %get-tuple-element.249, pred[]{:T(512)S(6)} %compare.7, bf16[32,8192]{1,0:T(8,128)(2,1)S(1)} %get-tuple-element.258, s32[]{:T(128)S(6)} %select_n.260), kind=kOutput, calls=%fused_computation.11.clone.1 | convolution fusion | flops 136445952 | bytes 602117 | tf_op jit(solution)/shard_map/while/body/eval_jaxpr/dot_general | solution.py:95
  77.7 3.2 %fusion.88 = f32[32,2048]{1,0:T(8,128)} fusion(s32[2048]{0:T(1024)S(1)} %bitcast.177, s32[1024]{0:T(1024)S(1)} %iota_add_fusion.2, f32[32,2048]{1,0:T(8,128)} %get-tuple-element.249, pred[]{:T(512)S(6)} %compare.7, bf16[32,8192]{1,0:T(8,128)(2,1)S(1)} %get-tuple-element.258, s32[]{:T(128)S(6)} %select_n.260), kind=kOutput, calls=%fused_computation.11.clone.1 | convolution fusion | flops 136445952 | bytes 602117 | tf_op jit(solution)/shard_map/while/body/eval_jaxpr/dot_general | solution.py:95
  80.9 3.2 %fusion.88 = f32[32,2048]{1,0:T(8,128)} fusion(s32[2048]{0:T(1024)S(1)} %bitcast.177, s32[1024]{0:T(1024)S(1)} %iota_add_fusion.2, f32[32,2048]{1,0:T(8,128)} %get-tuple-element.249, pred[]{:T(512)S(6)} %compare.7, bf16[32,8192]{1,0:T(8,128)(2,1)S(1)} %get-tuple-element.258, s32[]{:T(128)S(6)} %select_n.260), kind=kOutput, calls=%fused_computation.11.clone.1 | convolution fusion | flops 136445952 | bytes 602117 | tf_op jit(solution)/shard_map/while/body/eval_jaxpr/dot_general | solution.py:95
  84.1 3.2 %fusion.88 = f32[32,2048]{1,0:T(8,128)} fusion(s32[2048]{0:T(1024)S(1)} %bitcast.177, s32[1024]{0:T(1024)S(1)} %iota_add_fusion.2, f32[32,2048]{1,0:T(8,128)} %get-tuple-element.249, pred[]{:T(512)S(6)} %compare.7, bf16[32,8192]{1,0:T(8,128)(2,1)S(1)} %get-tuple-element.258, s32[]{:T(128)S(6)} %select_n.260), kind=kOutput, calls=%fused_computation.11.clone.1 | convolution fusion | flops 136445952 | bytes 602117 | tf_op jit(solution)/shard_map/while/body/eval_jaxpr/dot_general | solution.py:95
  87.3 3.2 %fusion.88 = f32[32,2048]{1,0:T(8,128)} fusion(s32[2048]{0:T(1024)S(1)} %bitcast.177, s32[1024]{0:T(1024)S(1)} %iota_add_fusion.2, f32[32,2048]{1,0:T(8,128)} %get-tuple-element.249, pred[]{:T(512)S(6)} %compare.7, bf16[32,8192]{1,0:T(8,128)(2,1)S(1)} %get-tuple-element.258, s32[]{:T(128)S(6)} %select_n.260), kind=kOutput, calls=%fused_computation.11.clone.1 | convolution fusion | flops 136445952 | bytes 602117 | tf_op jit(solution)/shard_map/while/body/eval_jaxpr/dot_general | solution.py:95
  95.0 3.6 %collective-permute-start.11 = (bf16[2,16,2,256]{3,1,0,2:T(8,128)(2,1)S(1)}, bf16[2,16,2,256]{3,1,0,2:T(8,128)(2,1)S(1)}, u32[]{:S(2)}, u32[]{:S(2)}) collective-permute-start(bf16[2,16,2,256]{3,1,0,2:T(8,128)(2,1)S(1)} %get-tuple-element.179), channel_id=1, source_target_pairs={{0,6},{1,7},{2,4},{3,5},{4,2},{5,3},{6,0},{7,1},{8,14},{9,15},{10,... | collective-permute-start | bytes 98312 | tf_op jit(solution)/shard_map/ppermute | solution.py:200
  119.3 4.5 %collective-permute-done.5 = bf16[16,16,256]{2,1,0:T(8,128)(2,1)S(1)} collective-permute-done((bf16[16,16,256]{2,1,0:T(8,128)(2,1)S(1)}, bf16[16,16,256]{2,1,0:T(8,128)(2,1)S(1)}, u32[]{:S(2)}, u32[]{:S(2)}) %collective-permute-start.5) | collective-permute-done | bytes 131104 | tf_op jit(solution)/shard_map/ppermute | solution.py:18
  129.1 5.3 %all-gather.2.cloned.1.call-done = bf16[64,16,2,256]{3,1,2,0:T(8,128)(2,1)} async-done(((bf16[16,16,2,256]{3,1,2,0:T(8,128)(2,1)}), bf16[64,16,2,256]{3,1,2,0:T(8,128)(2,1)}) %all-gather.2.cloned.1.call-update) | async-done | bytes 1048592 | tf_op jit(solution)/shard_map/all_gather | solution.py:210
  134.4 3.3 %gather_fusion.1 = bf16[128,16,2,256]{3,1,2,0:T(8,128)(2,1)} fusion(bf16[64,16,2,256]{3,1,2,0:T(8,128)(2,1)} %all-gather.2.cloned.1.call-done, s32[1024]{0:T(1024)S(1)} %pad_clamp_fusion), kind=kCustom, calls=%fused_computation.5 | custom fusion | bytes 4194816 | tf_op jit(solution)/shard_map/jit(_take)/gather | solution.py:211
  141.1 5.5 %all-to-all-start = ((bf16[16,16,2,256]{3,1,2,0:T(8,128)(2,1)}), bf16[16,16,2,256]{3,1,2,0:T(8,128)(2,1)S(1)}, u32[]{:S(2)}, u32[]{:S(2)}) async-start(bf16[16,16,2,256]{3,1,2,0:T(8,128)(2,1)} %pad_maximum_fusion.8), calls=%async_computation | async-start | bytes 524288 | tf_op jit(solution)/shard_map/all_to_all | solution.py:214
  150.3 5.6 %all-to-all-done = bf16[16,16,2,256]{3,1,2,0:T(8,128)(2,1)S(1)} async-done(((bf16[16,16,2,256]{3,1,2,0:T(8,128)(2,1)}), bf16[16,16,2,256]{3,1,2,0:T(8,128)(2,1)S(1)}, u32[]{:S(2)}, u32[]{:S(2)}) %all-to-all-start) | async-done | bytes 262176 | tf_op jit(solution)/shard_map/all_to_all | solution.py:214
  156.4 4.4 %add_convert_fusion = (bf16[2,8,16,1,2048]{4,3,2,1,0:T(2,128)(2,1)S(1)}, bf16[2,8,16,1,2048]{4,3,2,1,0:T(2,128)(2,1)S(1)}) fusion(f32[2,16,2048]{2,1,0:T(8,128)S(1)} %get-tuple-element.170, f32[8,2048]{1,0:T(8,128)S(1)} %get-tuple-element.186, f32[2,16,2048]{2,1,0:T(8,128)S(1)} %get-tuple-element.169, f32[8,2048]{1,0:T(8,128)S(1)} %get-tuple-element.185), kind=kLoop, calls=%fused_computation.34 | loop fusion | flops 4194304 | bytes 2752512 | tf_op jit(solution)/shard_map/convert.3
  160.8 5.2 %pad_maximum_fusion = bf16[2,8,16,2,2048]{4,3,2,1,0:T(2,128)(2,1)} fusion(bf16[2,8,16,1,2048]{4,3,2,1,0:T(2,128)(2,1)S(1)} %get-tuple-element.168, bf16[2,8,16,1,2048]{4,3,2,1,0:T(2,128)(2,1)S(1)} %get-tuple-element.167), kind=kLoop, calls=%fused_computation.30 | loop fusion | flops 4194304 | bytes 4194304 | tf_op jit(solution)/shard_map/stack | solution.py:76
  166.0 4.1 %convert_element_type.61 = bf16[512,2048]{1,0:T(8,128)(2,1)} reshape(bf16[2,8,16,2,2048]{4,3,2,1,0:T(2,128)(2,1)} %pad_maximum_fusion) | data formatting | bytes 4194304 | tf_op jit(solution)/shard_map/convert_element_type | solution.py:76
  170.2 3.7 %convolution_convert_fusion = bf16[512,512]{1,0:T(8,128)(2,1)} fusion(bf16[512,2048]{1,0:T(8,128)(2,1)} %convert_element_type.61, bf16[512,2048]{1,0:T(8,128)(2,1)S(1)} %copy-done), kind=kOutput, calls=%fused_computation.40 | convolution fusion | flops 1074003968 | bytes 4718592 | tf_op jit(solution)/shard_map/dot_general | solution.py:77
  (174 shorter events, 73.0 us)
Async XLA Ops:
  7.2 85.9 %copy-start = (bf16[512,2048]{1,0:T(8,128)(2,1)S(1)}, bf16[512,2048]{1,0:T(8,128)(2,1)}, u32[]{:S(2)}) copy-start(bf16[512,2048]{1,0:T(8,128)(2,1)} %param.27) | copy-start | bytes 6291460
  7.2 127.2 %all-gather.2.cloned.1.call-start = ((), (), s32[]{:S(2)}) async-start(), calls=%async_computation.1 | async-start | bytes 1310720 | tf_op jit(solution)/shard_map/all_gather | solution.py:210
  24.6 8.3 %collective-permute-start = (bf16[66,2,16,128]{3,2,1,0:T(8,128)(2,1)}, bf16[66,2,16,128]{3,2,1,0:T(8,128)(2,1)}, u32[]{:S(2)}, u32[]{:S(2)}) collective-permute-start(bf16[66,2,16,128]{3,2,1,0:T(8,128)(2,1)} %get-tuple-element.165), channel_id=1, source_target_pairs={{0,8},{8,16},{16,24},{1,9},{9,17},{17,25},{2,10},{10,18},{18,26},{... | collective-permute-start | bytes 1622024 | tf_op jit(solution)/shard_map/ppermute | solution.py:17
  27.9 5.5 %collective-permute-start.1 = (bf16[66,2,16,128]{3,2,1,0:T(8,128)(2,1)}, bf16[66,2,16,128]{3,2,1,0:T(8,128)(2,1)}, u32[]{:S(2)}, u32[]{:S(2)}) collective-permute-start(bf16[66,2,16,128]{3,2,1,0:T(8,128)(2,1)} %get-tuple-element.166), channel_id=1, source_target_pairs={{8,0},{16,8},{24,16},{9,1},{17,9},{25,17},{10,2},{18,10},{26,18},{... | collective-permute-start | bytes 1622024 | tf_op jit(solution)/shard_map/ppermute | solution.py:18
  37.8 11.8 %collective-permute-start.2 = (bf16[66,8,2,128]{3,2,1,0:T(2,128)(2,1)}, bf16[66,8,2,128]{3,2,1,0:T(2,128)(2,1)}, u32[]{:S(2)}, u32[]{:S(2)}) collective-permute-start(bf16[66,8,2,128]{3,2,1,0:T(2,128)(2,1)} %get-tuple-element.163), channel_id=1, source_target_pairs={{0,1},{1,2},{2,3},{3,4},{4,5},{5,6},{6,7},{8,9},{9,10},{10,11},{11... | collective-permute-start | bytes 811016 | tf_op jit(solution)/shard_map/ppermute | solution.py:17
  42.4 8.7 %collective-permute-start.3 = (bf16[66,8,2,128]{3,2,1,0:T(2,128)(2,1)}, bf16[66,8,2,128]{3,2,1,0:T(2,128)(2,1)}, u32[]{:S(2)}, u32[]{:S(2)}) collective-permute-start(bf16[66,8,2,128]{3,2,1,0:T(2,128)(2,1)} %get-tuple-element.164), channel_id=1, source_target_pairs={{1,0},{2,1},{3,2},{4,3},{5,4},{6,5},{7,6},{9,8},{10,9},{11,10},{12... | collective-permute-start | bytes 811016 | tf_op jit(solution)/shard_map/ppermute | solution.py:18
  65.8 26.6 %copy-start.14 = (bf16[128,512]{1,0:T(8,128)(2,1)S(1)}, bf16[128,512]{1,0:T(8,128)(2,1)}, u32[]{:S(2)}) copy-start(bf16[128,512]{1,0:T(8,128)(2,1)} %fusion.71) | copy-start | bytes 393220
  65.8 26.6 %copy-start.16 = (bf16[128,512]{1,0:T(8,128)(2,1)S(1)}, bf16[128,512]{1,0:T(8,128)(2,1)}, u32[]{:S(2)}) copy-start(bf16[128,512]{1,0:T(8,128)(2,1)} %get-tuple-element.181) | copy-start | bytes 393220
  65.8 26.6 %copy-start.18 = (bf16[128,512]{1,0:T(8,128)(2,1)S(1)}, bf16[128,512]{1,0:T(8,128)(2,1)}, u32[]{:S(2)}) copy-start(bf16[128,512]{1,0:T(8,128)(2,1)} %get-tuple-element.182) | copy-start | bytes 393220
  94.3 19.0 %copy-start.22 = (s32[16,4]{0,1:T(4,128)S(1)}, s32[16,4]{0,1:T(4,128)}, u32[]{:S(2)}) copy-start(s32[16,4]{0,1:T(4,128)} %broadcast_subtract_fusion) | copy-start | bytes 772
  94.3 19.1 %copy-start.21 = (pred[16,8]{1,0:T(8,128)(4,1)S(1)}, pred[16,8]{1,0:T(8,128)(4,1)}, u32[]{:S(2)}) copy-start(pred[16,8]{1,0:T(8,128)(4,1)} %copy.44) | copy-start | bytes 388
  95.0 18.8 %copy-start.10 = (bf16[2,16,16,128]{3,0,1,2:T(2,128)(2,1)S(1)}, bf16[2,16,16,128]{3,0,1,2:T(2,128)(2,1)}, u32[]{:S(2)}) copy-start(bf16[2,16,16,128]{3,0,1,2:T(2,128)(2,1)} %copy-done.9) | copy-start | bytes 393220
  95.0 21.7 %copy-start.26 = (s32[128]{0:T(128)S(1)}, s32[128]{0:T(128)}, u32[]{:S(2)}) copy-start(s32[128]{0:T(128)} %reshape.222) | copy-start | bytes 1540
  95.0 21.8 %copy-start.25 = (pred[16,8]{0,1:T(8,128)(4,1)S(1)}, pred[16,8]{0,1:T(8,128)(4,1)}, u32[]{:S(2)}) copy-start(pred[16,8]{0,1:T(8,128)(4,1)} %get-tuple-element.137) | copy-start | bytes 388
  95.0 17.5 %collective-permute-start.11 = (bf16[2,16,2,256]{3,1,0,2:T(8,128)(2,1)S(1)}, bf16[2,16,2,256]{3,1,0,2:T(8,128)(2,1)S(1)}, u32[]{:S(2)}, u32[]{:S(2)}) collective-permute-start(bf16[2,16,2,256]{3,1,0,2:T(8,128)(2,1)S(1)} %get-tuple-element.179), channel_id=1, source_target_pairs={{0,6},{1,7},{2,4},{3,5},{4,2},{5,3},{6,0},{7,1},{8,14},{9,15},{10,... | collective-permute-start | bytes 98312 | tf_op jit(solution)/shard_map/ppermute | solution.py:200
  98.7 13.9 %collective-permute-start.10 = (bf16[2,16,2,256]{3,1,0,2:T(8,128)(2,1)S(1)}, bf16[2,16,2,256]{3,1,0,2:T(8,128)(2,1)S(1)}, u32[]{:S(2)}, u32[]{:S(2)}) collective-permute-start(bf16[2,16,2,256]{3,1,0,2:T(8,128)(2,1)S(1)} %get-tuple-element.180), channel_id=1, source_target_pairs={{0,5},{1,4},{2,7},{3,6},{4,1},{5,0},{6,3},{7,2},{8,13},{9,12},{10,... | collective-permute-start | bytes 98312 | tf_op jit(solution)/shard_map/ppermute | solution.py:200
  99.4 13.1 %collective-permute-start.12 = (bf16[2,16,2,256]{3,1,0,2:T(8,128)(2,1)S(1)}, bf16[2,16,2,256]{3,1,0,2:T(8,128)(2,1)S(1)}, u32[]{:S(2)}, u32[]{:S(2)}) collective-permute-start(bf16[2,16,2,256]{3,1,0,2:T(8,128)(2,1)S(1)} %get-tuple-element.173), channel_id=1, source_target_pairs={{0,7},{1,6},{2,5},{3,4},{4,3},{5,2},{6,1},{7,0},{8,15},{9,14},{10,... | collective-permute-start | bytes 98312 | tf_op jit(solution)/shard_map/ppermute | solution.py:200
  101.6 3.9 %collective-permute-start.6 = (bf16[2,16,2,256]{3,1,0,2:T(8,128)(2,1)S(1)}, bf16[2,16,2,256]{3,1,0,2:T(8,128)(2,1)S(1)}, u32[]{:S(2)}, u32[]{:S(2)}) collective-permute-start(bf16[2,16,2,256]{3,1,0,2:T(8,128)(2,1)S(1)} %get-tuple-element.175), channel_id=1, source_target_pairs={{0,1},{1,0},{2,3},{3,2},{4,5},{5,4},{6,7},{7,6},{8,9},{9,8},{10,11... | collective-permute-start | bytes 98312 | tf_op jit(solution)/shard_map/ppermute | solution.py:200
  103.4 4.2 %collective-permute-start.7 = (bf16[2,16,2,256]{3,1,0,2:T(8,128)(2,1)S(1)}, bf16[2,16,2,256]{3,1,0,2:T(8,128)(2,1)S(1)}, u32[]{:S(2)}, u32[]{:S(2)}) collective-permute-start(bf16[2,16,2,256]{3,1,0,2:T(8,128)(2,1)S(1)} %get-tuple-element.176), channel_id=1, source_target_pairs={{0,2},{1,3},{2,0},{3,1},{4,6},{5,7},{6,4},{7,5},{8,10},{9,11},{10,... | collective-permute-start | bytes 98312 | tf_op jit(solution)/shard_map/ppermute | solution.py:200
  105.5 5.2 %collective-permute-start.8 = (bf16[2,16,2,256]{3,1,0,2:T(8,128)(2,1)S(1)}, bf16[2,16,2,256]{3,1,0,2:T(8,128)(2,1)S(1)}, u32[]{:S(2)}, u32[]{:S(2)}) collective-permute-start(bf16[2,16,2,256]{3,1,0,2:T(8,128)(2,1)S(1)} %get-tuple-element.177), channel_id=1, source_target_pairs={{0,3},{1,2},{2,1},{3,0},{4,7},{5,6},{6,5},{7,4},{8,11},{9,10},{10,... | collective-permute-start | bytes 98312 | tf_op jit(solution)/shard_map/ppermute | solution.py:200
  107.6 4.9 %collective-permute-start.9 = (bf16[2,16,2,256]{3,1,0,2:T(8,128)(2,1)S(1)}, bf16[2,16,2,256]{3,1,0,2:T(8,128)(2,1)S(1)}, u32[]{:S(2)}, u32[]{:S(2)}) collective-permute-start(bf16[2,16,2,256]{3,1,0,2:T(8,128)(2,1)S(1)} %get-tuple-element.178), channel_id=1, source_target_pairs={{0,4},{1,5},{2,6},{3,7},{4,0},{5,1},{6,2},{7,3},{8,12},{9,13},{10,... | collective-permute-start | bytes 98312 | tf_op jit(solution)/shard_map/ppermute | solution.py:200
  113.9 5.3 %collective-permute-start.4 = (bf16[16,16,256]{2,1,0:T(8,128)(2,1)S(1)}, bf16[16,16,256]{2,1,0:T(8,128)(2,1)S(1)}, u32[]{:S(2)}, u32[]{:S(2)}) collective-permute-start(bf16[16,16,256]{2,1,0:T(8,128)(2,1)S(1)} %reshape.177), channel_id=1, source_target_pairs={{0,1},{1,2},{2,3},{3,4},{4,5},{5,6},{6,7},{8,9},{9,10},{10,11},{11... | collective-permute-start | bytes 393224 | tf_op jit(solution)/shard_map/ppermute | solution.py:17
  116.9 6.9 %collective-permute-start.5 = (bf16[16,16,256]{2,1,0:T(8,128)(2,1)S(1)}, bf16[16,16,256]{2,1,0:T(8,128)(2,1)S(1)}, u32[]{:S(2)}, u32[]{:S(2)}) collective-permute-start(bf16[16,16,256]{2,1,0:T(8,128)(2,1)S(1)} %reshape.177), channel_id=1, source_target_pairs={{1,0},{2,1},{3,2},{4,3},{5,4},{6,5},{7,6},{9,8},{10,9},{11,10},{12... | collective-permute-start | bytes 393224 | tf_op jit(solution)/shard_map/ppermute | solution.py:18
  141.1 14.8 %all-to-all-start = ((bf16[16,16,2,256]{3,1,2,0:T(8,128)(2,1)}), bf16[16,16,2,256]{3,1,2,0:T(8,128)(2,1)S(1)}, u32[]{:S(2)}, u32[]{:S(2)}) async-start(bf16[16,16,2,256]{3,1,2,0:T(8,128)(2,1)} %pad_maximum_fusion.8), calls=%async_computation | async-start | bytes 524288 | tf_op jit(solution)/shard_map/all_to_all | solution.py:214
  (20 other events, 82.9 us)
Sparse Core Ops, SparseCore 0:
  113.5 20.8 all-gather.1
